TPU v7x, 32 devices: a whole 2x2x4 slice. The times are simulated.
32 devices in a mesh: row: 4 (over z), col: 8 (over y, x, core).
Axes of the slice: x: 2, y: 2, z: 4, core: 2. Of those that a mesh axis runs over, the one named last changes fastest.
Arguments:
- trailing: float32 [16384, 3072], P('row', 'col'), may hold values from -6 to 6
- leaf_vectors: float32 [16384, 256], P(('row', 'col')), may hold values from -1 to 1, as said below
- leaf_factor: float32 [1024, 256], P(('row', 'col')), may hold values from -1 to 2, as said below
- tree_vectors: float32 [1024, 256], P(('row', 'col')), may hold values from -1 to 1, as said below
- tree_factor: float32 [1024, 256], P(('row', 'col')), may hold values from -1 to 2, as said below
Outputs:
- updated: float32 [16384, 3072], P('row', 'col')
Inputs may be any that keep to these rules, and one draw needn't show every extreme that they name: `leaf_vectors`: in each row block of 4096 rows, row r < 256 of the block holds 1 in column r and 0 in every column after r. `leaf_factor`: each 256 x 256 block is upper triangular with its diagonal between 1 and 2. `tree_vectors`: each 256 x 256 block is upper triangular. `tree_factor`: each 256 x 256 block is upper triangular with its diagonal between 1 and 2.
All inputs are finite; a program needn't handle non-finite values.
Results may differ from a plain program's by a relative error of at most 0.0002.
Values sent between devices are 32-bit elements; how exact they have to be, the bound alone decides.
No kernel may reach another device: no remote copies, remote signals or barrier semaphores. Data moves between devices by JAX's collectives and lax.ppermute only.
A program may use at most 128 MiB of HBM per device.

v0:
```python
import jax
import jax.numpy as jnp
from jax import lax
from jax.sharding import PartitionSpec as P

highest = lax.Precision.HIGHEST
contract_rows = (((0,), (0,)), ((), ()))


def swapped(array, axis, apart):
    return lax.ppermute(array, axis, [(i, i ^ 1 << apart) for i in range(lax.axis_size(axis))])


def left_product(first, second):
    return lax.dot_general(
        first, second, contract_rows, precision=highest, preferred_element_type=jnp.float32
    )


def plain_product(first, second):
    return jnp.dot(first, second, precision=highest, preferred_element_type=jnp.float32)


def shards(trailing, leaf_vectors, leaf_factor, tree_vectors, tree_factor):
    panel_width = leaf_factor.shape[1]
    panel, block_factor, own_vectors, own_factor = (
        lax.all_gather(leaf_vectors, "col", axis=0, tiled=True),
        lax.all_gather(leaf_factor, "col", axis=0, tiled=True),
        lax.all_gather(tree_vectors, "col", axis=0, tiled=True),
        lax.all_gather(tree_factor, "col", axis=0, tiled=True),
    )
    weights = left_product(block_factor, left_product(panel, trailing))
    updated = trailing - plain_product(panel, weights)
    upper_rows = updated[:panel_width]
    lower_rows = updated[panel_width:]
    sections = lax.axis_size("row").bit_length() - 1
    position = lax.axis_index("row")
    pair_vectors, pair_factor = (
        lax.all_gather(own_vectors, "row", axis=0, tiled=True),
        lax.all_gather(own_factor, "row", axis=0, tiled=True),
    )
    current = upper_rows
    final_top = upper_rows
    for level_bit in range(sections):
        stride = 1 << level_bit
        partner_top = swapped(current, "row", level_bit)
        on_upper = position // stride % 2 == 1
        lower_group = jnp.where(on_upper, partner_top, current)
        upper_group = jnp.where(on_upper, current, partner_top)
        chosen = position // (2 * stride) * (2 * stride) + stride
        vectors = lax.dynamic_slice_in_dim(pair_vectors, chosen * panel_width, panel_width, 0)
        factor = lax.dynamic_slice_in_dim(pair_factor, chosen * panel_width, panel_width, 0)
        tree_weights = left_product(factor, lower_group + left_product(vectors, upper_group))
        final_top = jnp.where(
            position % (2 * stride) == stride,
            upper_group - plain_product(vectors, tree_weights),
            final_top,
        )
        current = lower_group - tree_weights
    final_top = jnp.where(position == 0, current, final_top)
    return jnp.concatenate([final_top, lower_rows], 0)


def solution(mesh):
    placed = (
        P("row", "col"),
        P(("row", "col"), None),
        P(("row", "col"), None),
        P(("row", "col"), None),
        P(("row", "col"), None),
    )
    return jax.shard_map(
        shards, mesh=mesh, in_specs=placed, out_specs=P("row", "col"), check_vma=False
    )
```

profile of v0, /device:TPU:0, one launch (start us, length us, event | category | flops | bytes accessed | tf_op | source)
XLA Modules:
  0.0 161.5 jit_solution(10669404419144354708)
XLA Ops:
  6.5 0.7 all-gather.4.cloned.1.call-update
  7.3 0.0 all-gather.8.cloned.1.call-start
  7.3 12.6 %all_gather.22 = f32[256,256]{1,0:T(8,128)} all-gather(f32[32,256]{1,0:T(8,128)} %param.8), channel_id=1, replica_groups=mesh['row'=4,'col'=8] {'col'}, dimensions={0}, use_global_device_ids=true | all-gather | bytes 294912 | tf_op jit(solution)/shard_map/all_gather | solution.py:29
  19.9 0.0 all-gather.8.cloned.1.call-update
  19.9 0.0 all-gather.6.cloned.1.call-start
  20.0 10.6 %all_gather.20 = f32[256,256]{1,0:T(8,128)} all-gather(f32[32,256]{1,0:T(8,128)} %param.9), channel_id=1, replica_groups=mesh['row'=4,'col'=8] {'col'}, dimensions={0}, use_global_device_ids=true | all-gather | bytes 294912 | tf_op jit(solution)/shard_map/all_gather | solution.py:30
  30.6 0.0 all-gather.6.cloned.1.call-update
  30.6 9.8 %all_gather.19 = f32[256,256]{1,0:T(8,128)S(1)} all-gather(f32[32,256]{1,0:T(8,128)} %param.7), channel_id=1, replica_groups=mesh['row'=4,'col'=8] {'col'}, dimensions={0}, use_global_device_ids=true | all-gather | bytes 294912 | tf_op jit(solution)/shard_map/all_gather | solution.py:28
  40.4 6.6 %copy.6 = f32[4096,384]{0,1:T(8,128)} copy(f32[4096,384]{1,0:T(8,128)} %param.5) | data formatting | bytes 12582912 | tf_op args[0]
  47.0 3.2 %all-gather.4.cloned.1.call-done = f32[4096,256]{1,0:T(8,128)} async-done(((f32[512,256]{1,0:T(8,128)}), f32[4096,256]{1,0:T(8,128)}) %all-gather.4.cloned.1.call-update) | async-done | bytes 4194320 | tf_op jit(solution)/shard_map/all_gather | solution.py:27
  50.2 9.9 %fusion.20 = f32[256,384]{1,0:T(8,128)S(1)} fusion(f32[4096,256]{1,0:T(8,128)} %all-gather.4.cloned.1.call-done, f32[4096,384]{1,0:T(8,128)} %param.5), kind=kOutput, calls=%fused_computation.29 | convolution fusion | flops 4831838208 | bytes 10878976 | tf_op jit(solution)/shard_map/dot_general | solution.py:15
  60.2 0.8 fusion.21
  61.0 6.0 %bitcast_subtract_fusion = f32[4096,384]{0,1:T(8,128)S(1)} fusion(f32[4096,384]{0,1:T(8,128)S(1)} %copy-done.1, f32[384,256]{1,0:T(8,128)S(1)} %fusion.21, f32[4096,256]{1,0:T(8,128)S(1)} %copy-done.2), kind=kOutput, calls=%fused_computation.1 | convolution fusion | flops 4833411072 | bytes 17170432 | tf_op jit(solution)/shard_map/dot_general | solution.py:21
  67.0 2.7 %copy-done = f32[4096,384]{0,1:T(8,128)} copy-done((f32[4096,384]{0,1:T(8,128)}, f32[4096,384]{0,1:T(8,128)S(1)}, u32[]{:S(2)}) %copy-start) | copy-done | bytes 6291480
  69.8 1.5 collective-permute-start
  71.3 10.8 %all-gather.8.cloned.1.call-done = f32[1024,256]{1,0:T(8,128)} async-done(((f32[256,256]{1,0:T(8,128)}), f32[1024,256]{1,0:T(8,128)}) %all-gather.8.cloned.1.call-update) | async-done | bytes 1048592 | tf_op jit(solution)/shard_map/all_gather | solution.py:39
  82.1 5.2 %collective-permute-done = f32[256,384]{0,1:T(8,128)S(1)} collective-permute-done((f32[256,384]{0,1:T(8,128)S(1)}, f32[256,384]{0,1:T(8,128)S(1)}, u32[]{:S(2)}, u32[]{:S(2)}) %collective-permute-start) | collective-permute-done | bytes 393248 | tf_op jit(solution)/shard_map/ppermute | solution.py:11
  87.3 1.7 %convolution_add_fusion.1 = f32[256,384]{0,1:T(8,128)S(1)} fusion(f32[1024,256]{1,0:T(8,128)} %all-gather.8.cloned.1.call-done, s32[]{:T(128)S(6)} %select_n.79, f32[256,384]{0,1:T(8,128)S(1)} %collective-permute-done, pred[]{:T(512)S(6)} %eq.20, f32[4096,384]{0,1:T(8,128)} %copy-done), kind=kOutput, calls=%fused_computation.7 | convolution fusion | flops 302284800 | bytes 2229760 | tf_op jit(solution)/shard_map/dot_general | solution.py:15
  89.0 26.9 %all-gather.6.cloned.1.call-done = f32[1024,256]{1,0:T(8,128)} async-done(((f32[256,256]{1,0:T(8,128)}), f32[1024,256]{1,0:T(8,128)}) %all-gather.6.cloned.1.call-update) | async-done | bytes 1048592 | tf_op jit(solution)/shard_map/all_gather | solution.py:40
  115.9 2.0 %fusion.4 = f32[256,384]{1,0:T(8,128)S(1)} fusion(f32[256,384]{0,1:T(8,128)S(1)} %convolution_add_fusion.1, f32[1024,256]{1,0:T(8,128)} %all-gather.6.cloned.1.call-done, s32[]{:T(128)S(6)} %select_n.79), kind=kOutput, calls=%fused_computation.11 | convolution fusion | flops 301989888 | bytes 1048580 | tf_op jit(solution)/shard_map/dot_general | solution.py:15
  117.9 0.2 copy.7
  118.0 1.1 fusion.12
  119.1 1.9 %collective-permute-start.1 = (f32[256,384]{0,1:T(8,128)S(1)}, f32[256,384]{0,1:T(8,128)S(1)}, u32[]{:S(2)}, u32[]{:S(2)}) collective-permute-start(f32[256,384]{0,1:T(8,128)S(1)} %fusion.12), channel_id=1, source_target_pairs={{0,16},{8,24},{16,0},{24,8},{1,17},{9,25},{17,1},{25,9},{2,18},{10... | collective-permute-start | bytes 1179656 | tf_op jit(solution)/shard_map/ppermute | solution.py:11
  121.0 5.6 %slice.9 = f32[3840,384]{0,1:T(8,128)} slice(f32[4096,384]{0,1:T(8,128)} %copy-done), slice={[256:4096], [0:384]} | slice | bytes 11796480 | tf_op jit(solution)/shard_map/slice | solution.py:35
  126.6 1.8 %fusion = f32[256,384]{0,1:T(8,128)S(1)} fusion(f32[256,384]{1,0:T(8,128)S(1)} %fusion.4, f32[1024,256]{1,0:T(8,128)S(1)} %copy-done.3, s32[]{:T(128)S(6)} %select_n.79, pred[]{:T(512)S(6)} %eq.20, f32[256,384]{0,1:T(8,128)S(1)} %collective-permute-done, f32[4096,384]{0,1:T(8,128)} %copy-done), kind=kOutput, calls=%fused_computation.3 | convolution fusion | flops 302284800 | bytes 1835013 | tf_op jit(solution)/shard_map/dot_general | solution.py:21
  128.4 10.5 %collective-permute-done.1 = f32[256,384]{0,1:T(8,128)S(1)} collective-permute-done((f32[256,384]{0,1:T(8,128)S(1)}, f32[256,384]{0,1:T(8,128)S(1)}, u32[]{:S(2)}, u32[]{:S(2)}) %collective-permute-start.1) | collective-permute-done | bytes 393248 | tf_op jit(solution)/shard_map/ppermute | solution.py:11
  138.9 0.5 convolution_add_fusion
  139.4 2.0 %fusion.2 = f32[256,384]{1,0:T(8,128)S(1)} fusion(f32[256,384]{0,1:T(8,128)S(1)} %convolution_add_fusion, f32[1024,256]{1,0:T(8,128)} %all-gather.6.cloned.1.call-done, s32[]{:T(128)S(6)} %select_n.83), kind=kOutput, calls=%fused_computation.9 | convolution fusion | flops 301989888 | bytes 1048580 | tf_op jit(solution)/shard_map/dot_general | solution.py:15
  141.4 0.2 copy.8
  141.6 0.8 subtract_select_fusion
  142.4 6.0 %pad_maximum_fusion = f32[4096,384]{0,1:T(8,128)} fusion(f32[3840,384]{0,1:T(8,128)} %slice.9, f32[256,384]{0,1:T(8,128)S(1)} %subtract_select_fusion), kind=kLoop, calls=%fused_computation | loop fusion | flops 1572864 | bytes 12582912 | tf_op jit(solution)/shard_map/concatenate | solution.py:61
  148.5 6.6 %copy.11 = f32[4096,384]{1,0:T(8,128)} copy(f32[4096,384]{0,1:T(8,128)} %pad_maximum_fusion) | data formatting | bytes 12582912 | tf_op jit(solution)/shard_map/concatenate | solution.py:61
  (9 shorter events, 0.0 us)
Async XLA Ops:
  6.5 43.7 %all-gather.4.cloned.1.call-start = ((), (), s32[]{:S(2)}) async-start(), calls=%async_computation | async-start | bytes 4718592 | tf_op jit(solution)/shard_map/all_gather | solution.py:27
  7.3 74.9 %all-gather.8.cloned.1.call-start = ((), (), s32[]{:S(2)}) async-start(), calls=%async_computation.2 | async-start | bytes 1310720 | tf_op jit(solution)/shard_map/all_gather | solution.py:39
  19.9 96.0 %all-gather.6.cloned.1.call-start = ((), (), s32[]{:S(2)}) async-start(), calls=%async_computation.1 | async-start | bytes 1310720 | tf_op jit(solution)/shard_map/all_gather | solution.py:40
  50.2 10.7 %copy-start.1 = (f32[4096,384]{0,1:T(8,128)S(1)}, f32[4096,384]{0,1:T(8,128)}, u32[]{:S(2)}) copy-start(f32[4096,384]{0,1:T(8,128)} %copy.6) | copy-start | bytes 18874372
  50.2 10.7 %copy-start.2 = (f32[4096,256]{1,0:T(8,128)S(1)}, f32[4096,256]{1,0:T(8,128)}, u32[]{:S(2)}) copy-start(f32[4096,256]{1,0:T(8,128)} %all-gather.4.cloned.1.call-done) | copy-start | bytes 12582916
  67.0 2.7 %copy-start = (f32[4096,384]{0,1:T(8,128)}, f32[4096,384]{0,1:T(8,128)S(1)}, u32[]{:S(2)}) copy-start(f32[4096,384]{0,1:T(8,128)S(1)} %bitcast_subtract_fusion) | copy-start | bytes 18874372
  69.8 17.5 %collective-permute-start = (f32[256,384]{0,1:T(8,128)S(1)}, f32[256,384]{0,1:T(8,128)S(1)}, u32[]{:S(2)}, u32[]{:S(2)}) collective-permute-start(f32[256,384]{0,1:T(8,128)S(1)} %slice.8), channel_id=1, source_target_pairs={{0,8},{8,0},{16,24},{24,16},{1,9},{9,1},{17,25},{25,17},{2,10},{10... | collective-permute-start | bytes 1179656 | tf_op jit(solution)/shard_map/ppermute | solution.py:11
  119.1 7.4 %copy-start.3 = (f32[1024,256]{1,0:T(8,128)S(1)}, f32[1024,256]{1,0:T(8,128)}, u32[]{:S(2)}) copy-start(f32[1024,256]{1,0:T(8,128)} %all-gather.8.cloned.1.call-done) | copy-start | bytes 3145732
  119.1 19.8 %collective-permute-start.1 = (f32[256,384]{0,1:T(8,128)S(1)}, f32[256,384]{0,1:T(8,128)S(1)}, u32[]{:S(2)}, u32[]{:S(2)}) collective-permute-start(f32[256,384]{0,1:T(8,128)S(1)} %fusion.12), channel_id=1, source_target_pairs={{0,16},{8,24},{16,0},{24,8},{1,17},{9,25},{17,1},{25,9},{2,18},{10... | collective-permute-start | bytes 1179656 | tf_op jit(solution)/shard_map/ppermute | solution.py:11
Sparse Core Ops, SparseCore 0:
  9.2 40.9 all-gather.3
  51.8 30.2 all-gather.7
  83.7 32.1 all-gather.5
where the time goes:
time: 162 us
  waiting for transfers between devices  57.4 us (35%)
  blocking collectives  33 us (20%)
  matrix products  25.5 us (16%)
  local copies, waits for them, and re-layouts  21.8 us (13%)
  between operations  13.2 us (8%)
  other arithmetic  7.11 us (4%)
  starting transfers between devices  3.49 us (2%)
    all_gather x1, waiting for transfers between devices, shards(): lax.all_gather(own_factor, 'row', axis=0, tiled=True)  26.9 us
    dot_general x6, matrix products, left_product(): lax.dot_general(first, second, contract_rows, precision=highest, preferre...  16.9 us
    ppermute x2, waiting for transfers between devices, swapped(): lax.ppermute(array, axis, [(i, i ^ 1 << apart) for i in range(lax.axis_si...  15.7 us
    all_gather x1, blocking collectives, shards(): lax.all_gather(tree_vectors, 'col', axis=0, tiled=True)  12.6 us
    all_gather x1, waiting for transfers between devices, shards(): lax.all_gather(own_vectors, 'row', axis=0, tiled=True)  10.8 us
    all_gather x1, blocking collectives, shards(): lax.all_gather(tree_factor, 'col', axis=0, tiled=True)  10.6 us
    all_gather x1, blocking collectives, shards(): lax.all_gather(leaf_factor, 'col', axis=0, tiled=True)  9.82 us
    unnamed x9, local copies, waits for them, and re-layouts  9.34 us
  transfers between devices with their start and end apart: 5, of which 5 were waited for; matrix products, arithmetic and copies ran while one was open for 20% of the time, Pallas kernels for 0%

commit v1 on v0

--- a/solution.py
+++ b/solution.py
@@ -5,6 +5,28 @@
 
 highest = lax.Precision.HIGHEST
 contract_rows = (((0,), (0,)), ((), ()))
+
+
+def laid_out(blocks, dim):
+    shape = list(blocks.shape[1:])
+    shape[dim] *= blocks.shape[0]
+    return jnp.moveaxis(blocks, 0, dim).reshape(shape)
+
+
+def ring_gather(x, axis, dim):
+    length = lax.axis_size(axis)
+    pairs = [(i, (i + 1) % length) for i in range(length)]
+    back = [(b, a) for a, b in pairs]
+    lower, upper = ([], [])
+    for step in range(length - 1):
+        if step % 2 == 0:
+            lower.append(lax.ppermute(lower[-1] if lower else x, axis, pairs))
+        else:
+            upper.append(lax.ppermute(upper[-1] if upper else x, axis, back))
+    tiles = jnp.stack([*lower[::-1], x, *upper])
+    shift = lax.axis_index(axis) - len(lower)
+    tiles = tiles[(jnp.arange(length) - shift) % length]
+    return laid_out(tiles, dim)
 
 
 def swapped(array, axis, apart):
@@ -37,7 +59,7 @@
     position = lax.axis_index("row")
     pair_vectors, pair_factor = (
         lax.all_gather(own_vectors, "row", axis=0, tiled=True),
-        lax.all_gather(own_factor, "row", axis=0, tiled=True),
+        ring_gather(own_factor, "row", 0),
     )
     current = upper_rows
     final_top = upper_rows

time: 162 us -> 135 us (0.83)
  waiting for transfers between devices: 57.4 us -> 26.7 us
  starting transfers between devices: 3.49 us -> 8.48 us
    all_gather x1 -> x0, waiting for transfers between devices: 26.9 us -> none  [shards(): lax.all_gather(own_factor, 'row', axis=0, tiled=True)]
    ppermute x0 -> x3, starting transfers between devices: none -> 4.42 us  [the longest x1 2.25 us: ring_gather(): upper.append(lax.ppermute(upper[-1] if upper else x, axis, back))]
    all_gather x1, waiting for transfers between devices: 3.21 us -> 0.45 us  [shards(): lax.all_gather(leaf_vectors, 'col', axis=0, tiled=True)]
    all_gather x1, blocking collectives: 12.6 us -> 10.6 us  [shards(): lax.all_gather(tree_vectors, 'col', axis=0, tiled=True)]
    dot_general x6, matrix products: 16.9 us -> 15 us  [left_product(): lax.dot_general(first, second, contract_rows, precision=highest, preferre...]
    unnamed x9 -> x11, local copies, waits for them, and re-layouts: 9.34 us -> 9.33 us
  transfers between devices with their start and end apart: 5 -> 7, of which waited for: 5 -> 4; matrix products, arithmetic and copies ran while one was open for 20% -> 23% of each run, Pallas kernels for 0% -> 0%
where the time goes in v1:
time: 135 us
  blocking collectives  31.5 us (23%)
  waiting for transfers between devices  26.7 us (20%)
  matrix products  24.6 us (18%)
  local copies, waits for them, and re-layouts  22.5 us (17%)
  between operations  13.6 us (10%)
  starting transfers between devices  8.48 us (6%)
  other arithmetic  7.22 us (5%)
    ppermute x2, waiting for transfers between devices, swapped(): lax.ppermute(array, axis, [(i, i ^ 1 << apart) for i in range(lax.axis_si...  15.5 us
    dot_general x6, matrix products, left_product(): lax.dot_general(first, second, contract_rows, precision=highest, preferre...  15 us
    all_gather x1, blocking collectives, shards(): lax.all_gather(tree_factor, 'col', axis=0, tiled=True)  11 us
    all_gather x1, blocking collectives, shards(): lax.all_gather(tree_vectors, 'col', axis=0, tiled=True)  10.6 us
    all_gather x1, waiting for transfers between devices, shards(): lax.all_gather(own_vectors, 'row', axis=0, tiled=True)  10.1 us
    all_gather x1, blocking collectives, shards(): lax.all_gather(leaf_factor, 'col', axis=0, tiled=True)  9.9 us
    dot_general x3, matrix products, plain_product(): jnp.dot(first, second, precision=highest, preferred_element_type=jnp.floa...  9.59 us
    unnamed x11, local copies, waits for them, and re-layouts  9.33 us
  transfers between devices with their start and end apart: 7, of which 4 were waited for; matrix products, arithmetic and copies ran while one was open for 23% of the time, Pallas kernels for 0%

profile of v1, /device:TPU:0, one launch (start us, length us, event | category | flops | bytes accessed | tf_op | source)
XLA Modules:
  0.0 134.6 jit_solution(289919218524241334)
XLA Ops:
  6.5 0.7 all-gather.3.cloned.1.call-update
  7.3 11.0 %all_gather.17 = f32[256,256]{1,0:T(8,128)S(1)} all-gather(f32[32,256]{1,0:T(8,128)} %param.9), channel_id=1, replica_groups=mesh['row'=4,'col'=8] {'col'}, dimensions={0}, use_global_device_ids=true | all-gather | bytes 294912 | tf_op jit(solution)/shard_map/all_gather | solution.py:52
  18.3 1.6 %collective-permute-start.1 = (f32[256,256]{1,0:T(8,128)S(1)}, f32[256,256]{1,0:T(8,128)S(1)}, u32[]{:S(2)}, u32[]{:S(2)}) collective-permute-start(f32[256,256]{1,0:T(8,128)S(1)} %all_gather.17), channel_id=1, source_target_pairs={{0,8},{8,16},{16,24},{24,0},{1,9},{9,17},{17,25},{25,1},{2,10},{10... | collective-permute-start | bytes 786440 | tf_op jit(solution)/shard_map/ppermute | solution.py:23
  19.9 2.2 %collective-permute-start.3 = (f32[256,256]{1,0:T(8,128)S(1)}, f32[256,256]{1,0:T(8,128)S(1)}, u32[]{:S(2)}, u32[]{:S(2)}) collective-permute-start(f32[256,256]{1,0:T(8,128)S(1)} %all_gather.17), channel_id=1, source_target_pairs={{8,0},{16,8},{24,16},{0,24},{9,1},{17,9},{25,17},{1,25},{10,2},{18... | collective-permute-start | bytes 786440 | tf_op jit(solution)/shard_map/ppermute | solution.py:25
  22.1 10.6 %all_gather.18 = f32[256,256]{1,0:T(8,128)} all-gather(f32[32,256]{1,0:T(8,128)} %param.8), channel_id=1, replica_groups=mesh['row'=4,'col'=8] {'col'}, dimensions={0}, use_global_device_ids=true | all-gather | bytes 294912 | tf_op jit(solution)/shard_map/all_gather | solution.py:51
  32.7 6.6 %copy.6 = f32[4096,384]{0,1:T(8,128)} copy(f32[4096,384]{1,0:T(8,128)} %param.5) | data formatting | bytes 12582912 | tf_op args[0]
  39.4 9.9 %all_gather.16 = f32[256,256]{1,0:T(8,128)S(1)} all-gather(f32[32,256]{1,0:T(8,128)S(1)} %copy-done.4), channel_id=1, replica_groups=mesh['row'=4,'col'=8] {'col'}, dimensions={0}, use_global_device_ids=true | all-gather | bytes 294912 | tf_op jit(solution)/shard_map/all_gather | solution.py:50
  49.3 0.6 collective-permute-start.2
  49.9 0.5 all-gather.3.cloned.1.call-done
  50.3 9.9 %fusion.22 = f32[256,384]{1,0:T(8,128)S(1)} fusion(f32[4096,256]{1,0:T(8,128)} %all-gather.3.cloned.1.call-done, f32[4096,384]{1,0:T(8,128)} %param.5), kind=kOutput, calls=%fused_computation.38 | convolution fusion | flops 4831838208 | bytes 10878976 | tf_op jit(solution)/shard_map/dot_general | solution.py:37
  60.2 0.8 fusion.23
  61.1 6.0 %bitcast_subtract_fusion = f32[4096,384]{0,1:T(8,128)S(1)} fusion(f32[4096,384]{0,1:T(8,128)S(1)} %copy-done.1, f32[384,256]{1,0:T(8,128)S(1)} %fusion.23, f32[4096,256]{1,0:T(8,128)S(1)} %copy-done.2), kind=kOutput, calls=%fused_computation.2 | convolution fusion | flops 4833411072 | bytes 17170432 | tf_op jit(solution)/shard_map/dot_general | solution.py:43
  67.1 2.7 %copy-done = f32[4096,384]{0,1:T(8,128)} copy-done((f32[4096,384]{0,1:T(8,128)}, f32[4096,384]{0,1:T(8,128)S(1)}, u32[]{:S(2)}) %copy-start) | copy-done | bytes 6291480
  69.8 1.6 %collective-permute-start = (f32[256,384]{0,1:T(8,128)S(1)}, f32[256,384]{0,1:T(8,128)S(1)}, u32[]{:S(2)}, u32[]{:S(2)}) collective-permute-start(f32[256,384]{0,1:T(8,128)S(1)} %slice.10), channel_id=1, source_target_pairs={{0,8},{8,0},{16,24},{24,16},{1,9},{9,1},{17,25},{25,17},{2,10},{10... | collective-permute-start | bytes 1179656 | tf_op jit(solution)/shard_map/ppermute | solution.py:33
  71.4 0.1 pad_maximum_fusion.1
  71.5 0.6 gather_fusion
  72.2 10.1 %all-gather.5.cloned.1.call-done = f32[1024,256]{1,0:T(8,128)} async-done(((f32[256,256]{1,0:T(8,128)}), f32[1024,256]{1,0:T(8,128)}) %all-gather.5.cloned.1.call-update) | async-done | bytes 1048592 | tf_op jit(solution)/shard_map/all_gather | solution.py:61
  82.2 5.2 %collective-permute-done = f32[256,384]{0,1:T(8,128)S(1)} collective-permute-done((f32[256,384]{0,1:T(8,128)S(1)}, f32[256,384]{0,1:T(8,128)S(1)}, u32[]{:S(2)}, u32[]{:S(2)}) %collective-permute-start) | collective-permute-done | bytes 393248 | tf_op jit(solution)/shard_map/ppermute | solution.py:33
  87.4 1.7 %convolution_add_fusion.1 = f32[256,384]{0,1:T(8,128)S(1)} fusion(f32[1024,256]{1,0:T(8,128)} %all-gather.5.cloned.1.call-done, s32[]{:T(128)S(6)} %select_n.104, f32[256,384]{0,1:T(8,128)S(1)} %collective-permute-done, pred[]{:T(512)S(6)} %eq.22, f32[4096,384]{0,1:T(8,128)} %copy-done), kind=kOutput, calls=%fused_computation.8 | convolution fusion | flops 302284800 | bytes 2229760 | tf_op jit(solution)/shard_map/dot_general | solution.py:37
  89.1 1.1 fusion.4
  90.1 0.2 copy.7
  90.3 1.1 fusion.12
  91.4 2.5 %collective-permute-start.4 = (f32[256,384]{0,1:T(8,128)S(1)}, f32[256,384]{0,1:T(8,128)S(1)}, u32[]{:S(2)}, u32[]{:S(2)}) collective-permute-start(f32[256,384]{0,1:T(8,128)S(1)} %fusion.12), channel_id=1, source_target_pairs={{0,16},{8,24},{16,0},{24,8},{1,17},{9,25},{17,1},{25,9},{2,18},{10... | collective-permute-start | bytes 1179656 | tf_op jit(solution)/shard_map/ppermute | solution.py:33
  93.9 5.7 %slice.11 = f32[3840,384]{0,1:T(8,128)} slice(f32[4096,384]{0,1:T(8,128)} %copy-done), slice={[256:4096], [0:384]} | slice | bytes 11796480 | tf_op jit(solution)/shard_map/slice | solution.py:57
  99.5 1.8 %fusion = f32[256,384]{0,1:T(8,128)S(1)} fusion(f32[256,384]{1,0:T(8,128)S(1)} %fusion.4, f32[1024,256]{1,0:T(8,128)S(1)} %copy-done.3, s32[]{:T(128)S(6)} %select_n.104, pred[]{:T(512)S(6)} %eq.22, f32[256,384]{0,1:T(8,128)S(1)} %collective-permute-done, f32[4096,384]{0,1:T(8,128)} %copy-done), kind=kOutput, calls=%fused_computation.4 | convolution fusion | flops 302284800 | bytes 1835013 | tf_op jit(solution)/shard_map/dot_general | solution.py:43
  101.3 10.3 %collective-permute-done.4 = f32[256,384]{0,1:T(8,128)S(1)} collective-permute-done((f32[256,384]{0,1:T(8,128)S(1)}, f32[256,384]{0,1:T(8,128)S(1)}, u32[]{:S(2)}, u32[]{:S(2)}) %collective-permute-start.4) | collective-permute-done | bytes 393248 | tf_op jit(solution)/shard_map/ppermute | solution.py:33
  111.6 0.5 convolution_add_fusion
  112.2 1.1 fusion.2
  113.2 0.2 copy.8
  113.4 1.8 %subtract_select_fusion = f32[256,384]{0,1:T(8,128)S(1)} fusion(f32[256,384]{0,1:T(8,128)S(1)} %copy.8, f32[256,384]{0,1:T(8,128)S(1)} %fusion, f32[256,384]{1,0:T(8,128)S(1)} %fusion.2, f32[1024,256]{1,0:T(8,128)} %all-gather.5.cloned.1.call-done, s32[]{:T(128)S(6)} %select_n.108, pred[]{:T(512)S(6)} %eq.23, pred[]{:T(512)S(6)} %eq.20, ...), kind=kOutput, calls=%fused_computation.10 | convolution fusion | flops 302579712 | bytes 2621447 | tf_op jit(solution)/shard_map/dot_general | solution.py:43
  115.2 6.0 %pad_maximum_fusion = f32[4096,384]{0,1:T(8,128)} fusion(f32[3840,384]{0,1:T(8,128)} %slice.11, f32[256,384]{0,1:T(8,128)S(1)} %subtract_select_fusion), kind=kLoop, calls=%fused_computation.1 | loop fusion | flops 1572864 | bytes 12582912 | tf_op jit(solution)/shard_map/concatenate | solution.py:83
  121.2 6.6 %copy.11 = f32[4096,384]{1,0:T(8,128)} copy(f32[4096,384]{0,1:T(8,128)} %pad_maximum_fusion) | data formatting | bytes 12582912 | tf_op jit(solution)/shard_map/concatenate | solution.py:83
  (18 shorter events, 0.1 us)
Async XLA Ops:
  6.5 43.8 %all-gather.3.cloned.1.call-start = ((), (), s32[]{:S(2)}) async-start(), calls=%async_computation | async-start | bytes 4718592 | tf_op jit(solution)/shard_map/all_gather | solution.py:49
  7.3 75.0 %all-gather.5.cloned.1.call-start = ((), (), s32[]{:S(2)}) async-start(), calls=%async_computation.1 | async-start | bytes 1310720 | tf_op jit(solution)/shard_map/all_gather | solution.py:61
  18.3 31.0 %collective-permute-start.1 = (f32[256,256]{1,0:T(8,128)S(1)}, f32[256,256]{1,0:T(8,128)S(1)}, u32[]{:S(2)}, u32[]{:S(2)}) collective-permute-start(f32[256,256]{1,0:T(8,128)S(1)} %all_gather.17), channel_id=1, source_target_pairs={{0,8},{8,16},{16,24},{24,0},{1,9},{9,17},{17,25},{25,1},{2,10},{10... | collective-permute-start | bytes 786440 | tf_op jit(solution)/shard_map/ppermute | solution.py:23
  19.9 51.5 %collective-permute-start.3 = (f32[256,256]{1,0:T(8,128)S(1)}, f32[256,256]{1,0:T(8,128)S(1)}, u32[]{:S(2)}, u32[]{:S(2)}) collective-permute-start(f32[256,256]{1,0:T(8,128)S(1)} %all_gather.17), channel_id=1, source_target_pairs={{8,0},{16,8},{24,16},{0,24},{9,1},{17,9},{25,17},{1,25},{10,2},{18... | collective-permute-start | bytes 786440 | tf_op jit(solution)/shard_map/ppermute | solution.py:25
  32.7 6.6 %copy-start.4 = (f32[32,256]{1,0:T(8,128)S(1)}, f32[32,256]{1,0:T(8,128)}, u32[]{:S(2)}) copy-start(f32[32,256]{1,0:T(8,128)} %param.7) | copy-start | bytes 98308
  49.3 22.2 %collective-permute-start.2 = (f32[256,256]{1,0:T(8,128)S(1)}, f32[256,256]{1,0:T(8,128)S(1)}, u32[]{:S(2)}, u32[]{:S(2)}) collective-permute-start(f32[256,256]{1,0:T(8,128)S(1)} %collective-permute-done.1), channel_id=1, source_target_pairs={{0,8},{8,16},{16,24},{24,0},{1,9},{9,17},{17,25},{25,1},{2,10},{10... | collective-permute-start | bytes 786440 | tf_op jit(solution)/shard_map/ppermute | solution.py:23
  50.3 10.7 %copy-start.1 = (f32[4096,384]{0,1:T(8,128)S(1)}, f32[4096,384]{0,1:T(8,128)}, u32[]{:S(2)}) copy-start(f32[4096,384]{0,1:T(8,128)} %copy.6) | copy-start | bytes 18874372
  50.3 10.7 %copy-start.2 = (f32[4096,256]{1,0:T(8,128)S(1)}, f32[4096,256]{1,0:T(8,128)}, u32[]{:S(2)}) copy-start(f32[4096,256]{1,0:T(8,128)} %all-gather.3.cloned.1.call-done) | copy-start | bytes 12582916
  67.1 2.7 %copy-start = (f32[4096,384]{0,1:T(8,128)}, f32[4096,384]{0,1:T(8,128)S(1)}, u32[]{:S(2)}) copy-start(f32[4096,384]{0,1:T(8,128)S(1)} %bitcast_subtract_fusion) | copy-start | bytes 18874372
  69.8 17.5 %collective-permute-start = (f32[256,384]{0,1:T(8,128)S(1)}, f32[256,384]{0,1:T(8,128)S(1)}, u32[]{:S(2)}, u32[]{:S(2)}) collective-permute-start(f32[256,384]{0,1:T(8,128)S(1)} %slice.10), channel_id=1, source_target_pairs={{0,8},{8,0},{16,24},{24,16},{1,9},{9,1},{17,25},{25,17},{2,10},{10... | collective-permute-start | bytes 1179656 | tf_op jit(solution)/shard_map/ppermute | solution.py:33
  91.4 20.3 %collective-permute-start.4 = (f32[256,384]{0,1:T(8,128)S(1)}, f32[256,384]{0,1:T(8,128)S(1)}, u32[]{:S(2)}, u32[]{:S(2)}) collective-permute-start(f32[256,384]{0,1:T(8,128)S(1)} %fusion.12), channel_id=1, source_target_pairs={{0,16},{8,24},{16,0},{24,8},{1,17},{9,25},{17,1},{25,9},{2,18},{10... | collective-permute-start | bytes 1179656 | tf_op jit(solution)/shard_map/ppermute | solution.py:33
  93.9 5.7 %copy-start.3 = (f32[1024,256]{1,0:T(8,128)S(1)}, f32[1024,256]{1,0:T(8,128)}, u32[]{:S(2)}) copy-start(f32[1024,256]{1,0:T(8,128)} %all-gather.5.cloned.1.call-done) | copy-start | bytes 3145732
Sparse Core Ops, SparseCore 0:
  9.2 41.0 all-gather.2
  51.9 30.2 all-gather.4
